TPU v7x, 256 devices: a whole 4x4x8 slice. The times are simulated.
256 devices in a mesh: tm: 16 (over z, core), height: 4 (over x), chan: 4 (over y).
Axes of the slice: x: 4, y: 4, z: 8, core: 2. Of those that a mesh axis runs over, the one named last changes fastest.
Arguments:
- frames: bfloat16 [32, 16, 256, 128], P('tm', 'height', 'chan'), may hold values from -6 to 6
- grad_out: bfloat16 [32, 16, 256, 128], P('tm', 'height', 'chan'), may hold values from -6 to 6
- weight_one: bfloat16 [256, 3, 3, 3, 256], P('chan'), may hold values from -0.078125 to 0.078125
- weight_two: bfloat16 [256, 3, 3, 3, 256], P('chan'), may hold values from -0.078125 to 0.078125
Outputs:
- grad_frames: bfloat16 [32, 16, 256, 128], P('tm', 'height', 'chan')
- grad_one: float32 [256, 3, 3, 3, 256], P('chan')
- grad_two: float32 [256, 3, 3, 3, 256], P('chan')
All inputs are finite; a program needn't handle non-finite values.
Results may differ from a plain program's by a relative error of at most 0.015.
Values may be sent and summed in bfloat16 or wider, within the bound.
No kernel may reach another device: no remote copies, remote signals or barrier semaphores. Data moves between devices by JAX's collectives and lax.ppermute only.
A program may use at most 128 MiB of HBM per device.

v0:
```python
import jax
import jax.numpy as jnp
from jax import lax
from jax.sharding import PartitionSpec as P


def passed_along(block, axis, distance):
    devices = range(lax.axis_size(axis))
    route = [(i - distance, i) for i in devices if i - distance in devices]
    return lax.ppermute(block, axis, route)


def extended(cells, sides, width):
    for axis, dim in sides:
        count = lax.axis_size(axis)
        ends = count - 1
        head = lax.slice_in_dim(cells, 0, width, axis=dim)
        tail = lax.slice_in_dim(cells, cells.shape[dim] - width, cells.shape[dim], axis=dim)
        cells = jnp.concatenate(
            [
                lax.ppermute(tail, axis, [(i, (i + 1) % count) for i in range(ends)]),
                cells,
                lax.ppermute(head, axis, [((i + 1) % count, i) for i in range(ends)]),
            ],
            axis=dim,
        )
    return cells


def product(form, left, right):
    return jnp.einsum(form, left, right, preferred_element_type=jnp.float32)


def shift_cols(block, offset):
    if offset == 0:
        return block
    edge = jnp.zeros(block.shape[:3] + (1,), block.dtype)
    if offset > 0:
        return jnp.concatenate([block[..., 1:], edge], 3)
    return jnp.concatenate([edge, block[..., :-1]], 3)


def forward_taps(padded, weight):
    frame_count = padded.shape[0] - 2
    row_count = padded.shape[1] - 2
    col_count = padded.shape[3]
    summed = jnp.zeros((frame_count, row_count, weight.shape[0], col_count), jnp.float32)
    for col_tap in range(3):
        partial_sum = jnp.zeros((frame_count, row_count, weight.shape[0], col_count), jnp.float32)
        for time_tap in range(3):
            for row_tap in range(3):
                window = padded[time_tap : time_tap + frame_count, row_tap : row_tap + row_count]
                partial_sum = partial_sum + product(
                    "frcw,oc->frow", window, weight[:, time_tap, row_tap, col_tap, :]
                )
        summed = summed + shift_cols(partial_sum, col_tap - 1)
    return summed


def backward_taps(padded, weight):
    frame_count = padded.shape[0] - 2
    row_count = padded.shape[1] - 2
    col_count = padded.shape[3]
    summed = jnp.zeros((frame_count, row_count, weight.shape[4], col_count), jnp.float32)
    for col_tap in range(3):
        partial_sum = jnp.zeros((frame_count, row_count, weight.shape[4], col_count), jnp.float32)
        for time_tap in range(3):
            for row_tap in range(3):
                window = padded[
                    2 - time_tap : 2 - time_tap + frame_count, 2 - row_tap : 2 - row_tap + row_count
                ]
                partial_sum = partial_sum + product(
                    "frow,oc->frcw", window, weight[:, time_tap, row_tap, col_tap, :]
                )
        summed = summed + shift_cols(partial_sum, 1 - col_tap)
    return summed


def forward_filter(padded, gradient):
    frame_count, row_count, out_width, col_count = gradient.shape
    moved = [shift_cols(gradient, 1 - col_tap) for col_tap in range(3)]
    pieces = []
    for time_tap in range(3):
        for row_tap in range(3):
            window = padded[time_tap : time_tap + frame_count, row_tap : row_tap + row_count]
            for col_tap in range(3):
                pieces.append(product("frcw,frow->oc", window, moved[col_tap]))
    return jnp.stack(pieces, 1).reshape(out_width, 3, 3, 3, padded.shape[2])


def backward_filter(source, padded):
    frame_count, row_count, in_width, col_count = source.shape
    moved = [shift_cols(padded, 1 - col_tap) for col_tap in range(3)]
    pieces = []
    for time_tap in range(3):
        for row_tap in range(3):
            for col_tap in range(3):
                window = moved[col_tap][
                    2 - time_tap : 2 - time_tap + frame_count, 2 - row_tap : 2 - row_tap + row_count
                ]
                pieces.append(product("frcw,frow->oc", source, window))
    return jnp.stack(pieces, 1).reshape(padded.shape[2], 3, 3, 3, in_width)


def on_device(frames, grad_out, weight_one, weight_two):
    earlier = passed_along(frames, "tm", 1)
    frames_time = jnp.concatenate([earlier, frames], 0)
    frames_rows = extended(frames_time, (("height", 1),), 1)
    frames_panel = lax.all_gather(frames_rows, "chan", axis=2, tiled=True)
    pre = forward_taps(frames_panel, weight_one)
    act = jax.nn.silu(pre).astype(jnp.bfloat16)
    later = passed_along(grad_out, "tm", -1)
    grads_time = jnp.concatenate([grad_out, later], 0)
    grads_padded = extended(grads_time, (("height", 1),), 1)
    act_full = lax.all_gather(act, "chan", axis=2, tiled=True)
    part_two = backward_filter(act_full, grads_padded)
    sigmoid_pre = jax.nn.sigmoid(pre)
    grad_act = lax.psum_scatter(
        backward_taps(grads_padded, weight_two), "chan", scatter_dimension=2, tiled=True
    )
    grad_pre = (grad_act * sigmoid_pre * (1.0 + pre * (1.0 - sigmoid_pre))).astype(jnp.bfloat16)
    pre_later = passed_along(grad_pre, "tm", -1)
    pre_time = jnp.concatenate([grad_pre, pre_later], 0)
    pre_padded = extended(pre_time, (("height", 1),), 1)
    grad_frames = lax.psum_scatter(
        backward_taps(pre_padded, weight_one).astype(jnp.bfloat16),
        "chan",
        scatter_dimension=2,
        tiled=True,
    )
    part_one = forward_filter(frames_panel, grad_pre)
    grad_one, grad_two = lax.psum((part_one, part_two), ("tm", "height"))
    return (grad_frames, grad_one, grad_two)


def solution(mesh):
    in_specs = (
        P("tm", "height", "chan", None),
        P("tm", "height", "chan", None),
        P("chan", None, None, None, None),
        P("chan", None, None, None, None),
    )
    out_specs = (
        P("tm", "height", "chan", None),
        P("chan", None, None, None, None),
        P("chan", None, None, None, None),
    )
    return jax.shard_map(
        on_device, mesh=mesh, in_specs=in_specs, out_specs=out_specs, check_vma=False
    )
```

profile of v0, /device:TPU:8, one launch (start us, length us, event | category | flops | bytes accessed | tf_op | source)
XLA Modules:
  0.0 437.9 jit_solution(17015021139338158347)
XLA Ops:
  7.2 1.4 collective-permute-start
  8.7 1.3 convolution_bitcast_fusion.21
  9.9 1.3 convolution_bitcast_fusion.25
  11.2 0.3 convolution_bitcast_fusion.23
  12.7 3.4 collective-permute-start.2
  16.1 1.3 collective-permute-start.1
  17.4 0.3 convolution_bitcast_fusion.26
  17.7 0.3 convolution_bitcast_fusion.22
  18.1 0.3 convolution_bitcast_fusion.24
  19.8 2.5 collective-permute-done.1
  22.6 0.3 convolution_bitcast_fusion.15
  22.9 0.3 convolution_bitcast_fusion.16
  23.2 0.3 convolution_bitcast_fusion.18
  23.6 0.3 convolution_bitcast_fusion.2
  23.9 0.3 convolution_bitcast_fusion.4
  24.2 1.1 fusion.1
  25.3 1.1 fusion.10
  26.4 1.2 slice_add_fusion
  27.6 1.1 convolution_bitcast_fusion.11
  28.7 1.1 convolution_bitcast_fusion.12
  29.8 1.1 convolution_bitcast_fusion.8
  30.9 1.1 convolution_bitcast_fusion.9
  32.0 1.1 convolution_bitcast_fusion.7
  33.1 1.6 fusion.36
  34.6 1.3 copy.128
  36.0 3.0 collective-permute-start.3
  39.1 1.0 collective-permute-done.3
  40.1 3.4 collective-permute-start.4
  43.5 1.3 collective-permute-start.5
  44.8 0.6 collective-permute-done.4
  45.4 4.3 collective-permute-done.5
  49.7 0.8 pad_maximum_fusion
  50.7 0.6 dynamic-slice
  52.2 37.8 %all-reduce.17.cloned.1.call-done = f32[2,4,256,128]{3,1,0,2:T(4,128)} async-done(((f32[2,4,256,128]{3,1,0,2:T(4,128)}), f32[2,4,256,128]{3,1,0,2:T(4,128)}) %all-reduce.17.cloned.1.call-update) | async-done | bytes 1048592
  90.0 1.7 constant_dynamic-slice_fusion.1
  91.7 30.6 %all-gather.2.cloned.1.call-done = bf16[4,6,256,128]{3,2,1,0:T(8,128)(2,1)} async-done(((bf16[4,6,64,128]{3,2,1,0:T(8,128)(2,1)}), bf16[4,6,256,128]{3,2,1,0:T(8,128)(2,1)}) %all-gather.2.cloned.1.call-update) | async-done | bytes 1572880 | tf_op jit(solution)/shard_map/all_gather | solution.py:109
  122.3 1.4 fusion.148
  123.7 1.3 convolution_add_fusion.13
  125.1 1.0 convolution_add_fusion.12
  126.1 1.0 convolution_add_fusion.11
  132.7 1.3 collective-permute-start.6
  135.1 13.3 %all_gather.7 = bf16[2,4,256,128]{3,1,0,2:T(4,128)(2,1)S(1)} all-gather(bf16[2,4,64,128]{3,1,0,2:T(4,128)(2,1)S(1)} %copy.131), channel_id=1, replica_groups=mesh['tm'=16,'height'=4,'chan'=4] {'chan'}, dimensions={2}, use_global_device_ids=true | all-gather | bytes 655360 | tf_op jit(solution)/shard_map/all_gather | solution.py:115
  163.1 3.4 collective-permute-start.8
  166.5 1.5 collective-permute-start.7
  170.7 2.0 collective-permute-done.7
  173.3 0.6 fusion.33
  173.9 0.3 fusion.27
  175.3 0.3 fusion.193
  175.6 0.3 fusion.228
  176.3 0.3 fusion.220
  176.6 0.3 fusion.217
  177.0 0.6 fusion.17
  177.9 0.6 fusion.26
  178.4 0.4 fusion.37
  178.8 1.1 copy.130
  180.0 0.9 fusion.72
  180.9 0.9 fusion.71
  181.8 0.9 fusion.70
  182.8 45.5 %all-reduce.19.cloned.1.call-done = bf16[2,4,256,128]{3,1,0,2:T(4,128)(2,1)} async-done(((bf16[2,4,256,128]{3,1,0,2:T(4,128)(2,1)}), bf16[2,4,256,128]{3,1,0,2:T(4,128)(2,1)}) %all-reduce.19.cloned.1.call-update) | async-done | bytes 524304
  228.3 0.9 constant_dynamic-slice_fusion
  229.2 0.7 copy.159
  229.9 197.3 %all-reduce.21.cloned.1.call-done = (f32[64,3,3,3,256]{4,0,3,2,1:T(8,128)}, f32[64,3,3,3,256]{4,0,3,2,1:T(8,128)}) async-done(((f32[64,3,3,3,256]{4,0,3,2,1:T(8,128)}, f32[64,3,3,3,256]{4,0,3,2,1:T(8,128)}), (f32[64,3,3,3,256]{4,0,3,2,1:T(8,128)}, f32[64,3,3,3,256]{4,0,3,2,1:T(8,128)})) %all-reduce.21.cloned.1.call-update) | async-done | bytes 3538960 | tf_op jit(solution)/shard_map/psum | solution.py:132
  427.2 3.0 copy.391
  430.2 1.2 copy.392
  (145 shorter events, 29.5 us)
Async XLA Ops:
  7.2 4.1 copy-start.2
  7.2 4.1 copy-start.6
  7.2 82.9 %all-reduce.17.cloned.1.call-start = ((), (), s32[]{:S(2)}) async-start(), calls=%async_computation.1 | async-start | bytes 2097152
  7.2 4.4 collective-permute-start
  12.7 5.8 %collective-permute-start.2 = (bf16[4,1,64,128]{3,2,1,0:T(8,128)(2,1)S(1)}, bf16[4,1,64,128]{3,2,1,0:T(8,128)(2,1)S(1)}, u32[]{:S(2)}, u32[]{:S(2)}) collective-permute-start(bf16[4,1,64,128]{3,2,1,0:T(8,128)(2,1)S(1)} %get-tuple-element.20), channel_id=1, source_target_pairs={{0,4},{4,8},{8,12},{1,5},{5,9},{9,13},{2,6},{6,10},{10,14},{3,7},{... | collective-permute-start | bytes 196616 | tf_op jit(solution)/shard_map/ppermute | solution.py:21
  16.1 6.2 %collective-permute-start.1 = (bf16[4,1,64,128]{3,2,1,0:T(8,128)(2,1)S(1)}, bf16[4,1,64,128]{3,2,1,0:T(8,128)(2,1)S(1)}, u32[]{:S(2)}, u32[]{:S(2)}) collective-permute-start(bf16[4,1,64,128]{3,2,1,0:T(8,128)(2,1)S(1)} %get-tuple-element.19), channel_id=1, source_target_pairs={{4,0},{8,4},{12,8},{5,1},{9,5},{13,9},{6,2},{10,6},{14,10},{7,3},{... | collective-permute-start | bytes 196616 | tf_op jit(solution)/shard_map/ppermute | solution.py:23
  34.6 1.4 copy-start.8
  36.0 14.8 %copy-start.9 = (u32[256]{0:T(256)S(1)}, u32[256]{0:T(256)}, u32[]{:S(2)}) copy-start(u32[256]{0:T(256)} %constant.34) | copy-start | bytes 3076
  36.0 86.3 %all-gather.2.cloned.1.call-start = ((), (), s32[]{:S(2)}) async-start(), calls=%async_computation | async-start | bytes 1966080 | tf_op jit(solution)/shard_map/all_gather | solution.py:109
  36.0 4.0 collective-permute-start.3
  40.1 5.3 %collective-permute-start.4 = (bf16[4,1,64,128]{3,2,1,0:T(8,128)(2,1)S(1)}, bf16[4,1,64,128]{3,2,1,0:T(8,128)(2,1)S(1)}, u32[]{:S(2)}, u32[]{:S(2)}) collective-permute-start(bf16[4,1,64,128]{3,2,1,0:T(8,128)(2,1)S(1)} %get-tuple-element.17), channel_id=1, source_target_pairs={{0,4},{4,8},{8,12},{1,5},{5,9},{9,13},{2,6},{6,10},{10,14},{3,7},{... | collective-permute-start | bytes 196616 | tf_op jit(solution)/shard_map/ppermute | solution.py:21
  43.5 6.2 %collective-permute-start.5 = (bf16[4,1,64,128]{3,2,1,0:T(8,128)(2,1)S(1)}, bf16[4,1,64,128]{3,2,1,0:T(8,128)(2,1)S(1)}, u32[]{:S(2)}, u32[]{:S(2)}) collective-permute-start(bf16[4,1,64,128]{3,2,1,0:T(8,128)(2,1)S(1)} %get-tuple-element.18), channel_id=1, source_target_pairs={{4,0},{8,4},{12,8},{5,1},{9,5},{13,9},{6,2},{10,6},{14,10},{7,3},{... | collective-permute-start | bytes 196616 | tf_op jit(solution)/shard_map/ppermute | solution.py:23
  50.5 177.8 %all-reduce.19.cloned.1.call-start = ((), (), s32[]{:S(2)}) async-start(), calls=%async_computation.2 | async-start | bytes 1048576
  122.3 2.8 copy-start
  123.7 3.3 copy-start.1
  131.3 1.0 copy-start.7
  132.7 30.3 %collective-permute-start.6 = (bf16[2,4,64,128]{3,2,1,0:T(8,128)(2,1)S(1)}, bf16[2,4,64,128]{3,2,1,0:T(8,128)(2,1)S(1)}, u32[]{:S(2)}, u32[]{:S(2)}) collective-permute-start(bf16[2,4,64,128]{3,2,1,0:T(8,128)(2,1)S(1)} %get-tuple-element.14), channel_id=1, source_target_pairs={{16,0},{32,16},{48,32},{64,48},{80,64},{96,80},{112,96},{128,112},... | collective-permute-start | bytes 393224 | tf_op jit(solution)/shard_map/ppermute | solution.py:10
  156.1 1.4 copy-start.3
  163.0 6.0 %copy-start.5 = (f32[64,27,256]{2,0,1:T(8,128)}, f32[64,27,256]{2,0,1:T(8,128)S(1)}, u32[]{:S(2)}) copy-start(f32[64,27,256]{2,0,1:T(8,128)S(1)} %fusion.73) | copy-start | bytes 5308420
  163.1 6.9 %collective-permute-start.8 = (bf16[4,1,64,128]{3,2,1,0:T(8,128)(2,1)S(1)}, bf16[4,1,64,128]{3,2,1,0:T(8,128)(2,1)S(1)}, u32[]{:S(2)}, u32[]{:S(2)}) collective-permute-start(bf16[4,1,64,128]{3,2,1,0:T(8,128)(2,1)S(1)} %get-tuple-element.15), channel_id=1, source_target_pairs={{0,4},{4,8},{8,12},{1,5},{5,9},{9,13},{2,6},{6,10},{10,14},{3,7},{... | collective-permute-start | bytes 196616 | tf_op jit(solution)/shard_map/ppermute | solution.py:21
  166.5 6.2 %collective-permute-start.7 = (bf16[4,1,64,128]{3,2,1,0:T(8,128)(2,1)S(1)}, bf16[4,1,64,128]{3,2,1,0:T(8,128)(2,1)S(1)}, u32[]{:S(2)}, u32[]{:S(2)}) collective-permute-start(bf16[4,1,64,128]{3,2,1,0:T(8,128)(2,1)S(1)} %get-tuple-element.16), channel_id=1, source_target_pairs={{4,0},{8,4},{12,8},{5,1},{9,5},{13,9},{6,2},{10,6},{14,10},{7,3},{... | collective-permute-start | bytes 196616 | tf_op jit(solution)/shard_map/ppermute | solution.py:23
  179.9 247.2 %all-reduce.21.cloned.1.call-start = ((), (), s32[]{:S(2)}) async-start(), calls=%async_computation.3 | async-start | bytes 7077888 | tf_op jit(solution)/shard_map/psum | solution.py:132
  427.2 3.0 copy-start.4
Sparse Core Ops, SparseCore 0:
  36.1 53.8 all-reduce.16
  92.6 29.7 all-gather.1
  180.1 48.1 all-reduce.18
  232.6 194.5 all-reduce.20
where the time goes:
time: 439 us; the launch traced here: 438 us
  waiting for transfers between devices  322 us (73%)
  matrix products  53.8 us (12%)
  starting transfers between devices  20.4 us (5%)
  between operations  15.3 us (3%)
  blocking collectives  13.3 us (3%)
  local copies, waits for them, and re-layouts  11.5 us (3%)
    psum x1, waiting for transfers between devices, on_device(): grad_one, grad_two = lax.psum((part_one, part_two), ('tm', 'height'))  197 us
    unnamed x6, waiting for transfers between devices  83.4 us
    dot_general x135, matrix products, product(): return jnp.einsum(form, left, right, preferred_element_type=jnp.float32)  53.8 us
    all_gather x1, waiting for transfers between devices, on_device(): frames_panel = lax.all_gather(frames_rows, 'chan', axis=2, tiled=True)  30.6 us
    all_gather x1, blocking collectives, on_device(): act_full = lax.all_gather(act, 'chan', axis=2, tiled=True)  13.3 us
    ppermute x3, starting transfers between devices, extended(): lax.ppermute(tail, axis, [(i, (i + 1) % count) for i in range(ends)])  10.2 us
  transfers between devices with their start and end apart: 13, of which 9 were waited for; matrix products, arithmetic and copies ran while one was open for 7% of the time, Pallas kernels for 0%

commit v1 on v0

--- a/solution.py
+++ b/solution.py
@@ -112,7 +112,9 @@
     later = passed_along(grad_out, "tm", -1)
     grads_time = jnp.concatenate([grad_out, later], 0)
     grads_padded = extended(grads_time, (("height", 1),), 1)
-    act_full = lax.all_gather(act, "chan", axis=2, tiled=True)
+    act_full = jnp.concatenate(
+        lax.all_to_all(jnp.stack([act] * lax.axis_size("chan")), "chan", 0, 0), axis=2
+    )
     part_two = backward_filter(act_full, grads_padded)
     sigmoid_pre = jax.nn.sigmoid(pre)
     grad_act = lax.psum_scatter(

time: 439 us -> 424 us (0.966)
  blocking collectives: 13.3 us -> 0 us
  waiting for transfers between devices: 322 us -> 316 us
  starting transfers between devices: 20.4 us -> 26 us
  matrix products: 53.8 us -> 48.8 us
    all_gather x1 -> x0, blocking collectives: 13.3 us -> none  [on_device(): act_full = lax.all_gather(act, 'chan', axis=2, tiled=True)]
    unnamed x6, waiting for transfers between devices: 83.4 us -> 76.6 us
    all_to_all x0 -> x1, starting transfers between devices: none -> 5.7 us  [on_device(): lax.all_to_all(jnp.stack([act] * lax.axis_size('chan')), 'chan', 0, 0)]
    dot_general x135, matrix products: 53.8 us -> 48.8 us  [product(): return jnp.einsum(form, left, right, preferred_element_type=jnp.float32)]
    unnamed x28 -> x34, local copies, waits for them, and re-layouts: 8.45 us -> 10.4 us
  transfers between devices with their start and end apart: 13 -> 14, of which waited for: 9 -> 9; matrix products, arithmetic and copies ran while one was open for 7% -> 10% of each run, Pallas kernels for 0% -> 0%
where the time goes in v1:
time: 424 us; the launch traced here: 423 us
  waiting for transfers between devices  316 us (75%)
  matrix products  48.8 us (12%)
  starting transfers between devices  26 us (6%)
  local copies, waits for them, and re-layouts  15.4 us (4%)
  between operations  15.3 us (4%)
    psum x1, waiting for transfers between devices, on_device(): grad_one, grad_two = lax.psum((part_one, part_two), ('tm', 'height'))  197 us
    unnamed x6, waiting for transfers between devices  76.6 us
    dot_general x135, matrix products, product(): return jnp.einsum(form, left, right, preferred_element_type=jnp.float32)  48.8 us
    all_gather x1, waiting for transfers between devices, on_device(): frames_panel = lax.all_gather(frames_rows, 'chan', axis=2, tiled=True)  31.3 us
    unnamed x34, local copies, waits for them, and re-layouts  10.4 us
    ppermute x3, starting transfers between devices, extended(): lax.ppermute(tail, axis, [(i, (i + 1) % count) for i in range(ends)])  10.2 us
    ppermute x3, waiting for transfers between devices, extended(): lax.ppermute(head, axis, [((i + 1) % count, i) for i in range(ends)])  8.97 us
  transfers between devices with their start and end apart: 14, of which 9 were waited for; matrix products, arithmetic and copies ran while one was open for 10% of the time, Pallas kernels for 0%

profile of v1, /device:TPU:8, one launch (start us, length us, event | category | flops | bytes accessed | tf_op | source)
XLA Modules:
  0.0 423.1 jit_solution(4822273328120684125)
XLA Ops:
  7.2 1.4 collective-permute-start
  8.7 1.3 convolution_bitcast_fusion.21
  9.9 1.3 convolution_bitcast_fusion.25
  11.2 0.3 convolution_bitcast_fusion.23
  12.7 3.4 collective-permute-start.2
  16.1 1.3 collective-permute-start.1
  17.4 0.3 convolution_bitcast_fusion.26
  17.7 0.3 convolution_bitcast_fusion.22
  18.1 0.3 convolution_bitcast_fusion.24
  19.8 2.5 collective-permute-done.1
  22.6 0.3 convolution_bitcast_fusion.15
  22.9 0.3 convolution_bitcast_fusion.16
  23.2 0.3 convolution_bitcast_fusion.18
  23.6 0.3 convolution_bitcast_fusion.2
  23.9 0.3 convolution_bitcast_fusion.4
  24.9 1.2 slice_add_fusion
  26.1 0.3 convolution_bitcast_fusion.11
  26.5 0.3 convolution_bitcast_fusion.12
  26.8 0.3 convolution_bitcast_fusion.8
  27.1 0.3 convolution_bitcast_fusion.9
  27.5 0.3 convolution_bitcast_fusion.7
  27.8 0.7 fusion.36
  28.5 1.3 copy.102
  29.9 3.0 collective-permute-start.3
  32.9 1.0 collective-permute-done.3
  34.0 3.4 collective-permute-start.4
  37.4 1.5 collective-permute-start.5
  38.8 0.4 collective-permute-done.4
  39.3 4.3 %collective-permute-done.5 = bf16[4,1,64,128]{3,2,1,0:T(8,128)(2,1)S(1)} collective-permute-done((bf16[4,1,64,128]{3,2,1,0:T(8,128)(2,1)S(1)}, bf16[4,1,64,128]{3,2,1,0:T(8,128)(2,1)S(1)}, u32[]{:S(2)}, u32[]{:S(2)}) %collective-permute-start.5) | collective-permute-done | bytes 65568 | tf_op jit(solution)/shard_map/ppermute | solution.py:23
  43.5 0.8 pad_maximum_fusion
  44.4 0.6 dynamic-slice
  45.9 38.0 %all-reduce.17.cloned.1.call-done = f32[2,4,256,128]{3,1,0,2:T(4,128)} async-done(((f32[2,4,256,128]{3,1,0,2:T(4,128)}), f32[2,4,256,128]{3,1,0,2:T(4,128)}) %all-reduce.17.cloned.1.call-update) | async-done | bytes 1048592
  83.9 1.0 constant_dynamic-slice_fusion.1
  84.9 31.3 %all-gather.2.cloned.1.call-done = bf16[4,6,256,128]{3,2,1,0:T(8,128)(2,1)} async-done(((bf16[4,6,64,128]{3,2,1,0:T(8,128)(2,1)}), bf16[4,6,256,128]{3,2,1,0:T(8,128)(2,1)}) %all-gather.2.cloned.1.call-update) | async-done | bytes 1572880 | tf_op jit(solution)/shard_map/all_gather | solution.py:109
  116.2 1.4 fusion.148
  117.6 1.3 convolution_add_fusion.13
  119.0 1.0 convolution_add_fusion.12
  119.9 1.0 convolution_add_fusion.11
  126.2 1.3 collective-permute-start.6
  127.5 1.3 fusion.238
  128.8 1.3 fusion.190
  130.1 1.3 fusion.214
  131.4 0.9 stack.203
  132.3 5.7 %all-to-all-start = ((bf16[4,2,4,64,128]{4,3,2,1,0:T(8,128)(2,1)}), bf16[4,2,4,64,128]{4,3,2,1,0:T(8,128)(2,1)}, u32[]{:S(2)}, u32[]{:S(2)}) async-start(bf16[4,2,4,64,128]{4,3,2,1,0:T(8,128)(2,1)} %stack.203), calls=%async_computation | async-start | bytes 1048576 | tf_op jit(solution)/shard_map/all_to_all | solution.py:116
  145.8 3.4 collective-permute-start.8
  149.2 1.5 collective-permute-start.7
  152.1 0.3 fusion.231
  153.4 2.2 collective-permute-done.7
  158.3 0.3 fusion.220
  159.2 0.6 fusion.33
  160.1 0.9 copy-done.2
  161.0 0.6 fusion.17
  161.6 0.7 copy-done.1
  162.2 0.6 fusion.26
  163.2 0.4 fusion.37
  163.6 1.1 copy.104
  164.8 1.1 copy.105
  173.7 1.2 copy-done.7
  174.9 38.5 %all-reduce.19.cloned.1.call-done = bf16[2,4,256,128]{3,1,0,2:T(4,128)(2,1)} async-done(((bf16[2,4,256,128]{3,1,0,2:T(4,128)(2,1)}), bf16[2,4,256,128]{3,1,0,2:T(4,128)(2,1)}) %all-reduce.19.cloned.1.call-update) | async-done | bytes 524304
  213.4 0.9 constant_dynamic-slice_fusion
  214.4 0.7 copy.106
  215.0 197.3 %all-reduce.21.cloned.1.call-done = (f32[64,3,3,3,256]{4,0,3,2,1:T(8,128)}, f32[64,3,3,3,256]{4,0,3,2,1:T(8,128)}) async-done(((f32[64,3,3,3,256]{4,0,3,2,1:T(8,128)}, f32[64,3,3,3,256]{4,0,3,2,1:T(8,128)}), (f32[64,3,3,3,256]{4,0,3,2,1:T(8,128)}, f32[64,3,3,3,256]{4,0,3,2,1:T(8,128)})) %all-reduce.21.cloned.1.call-update) | async-done | bytes 3538960 | tf_op jit(solution)/shard_map/psum | solution.py:134
  412.3 3.0 copy.284
  415.3 1.2 copy.285
  (153 shorter events, 30.6 us)
Async XLA Ops:
  7.2 4.1 copy-start.6
  7.2 4.1 copy-start.10
  7.2 76.7 %all-reduce.17.cloned.1.call-start = ((), (), s32[]{:S(2)}) async-start(), calls=%async_computation.2 | async-start | bytes 2097152
  7.2 4.4 %collective-permute-start = (bf16[2,4,64,128]{3,2,1,0:T(8,128)(2,1)}, bf16[2,4,64,128]{3,2,1,0:T(8,128)(2,1)S(1)}, u32[]{:S(2)}, u32[]{:S(2)}) collective-permute-start(bf16[2,4,64,128]{3,2,1,0:T(8,128)(2,1)} %param.5), channel_id=1, source_target_pairs={{16,0},{32,16},{48,32},{64,48},{80,64},{96,80},{112,96},{128,112},... | collective-permute-start | bytes 393224 | tf_op jit(solution)/shard_map/ppermute | solution.py:10
  12.7 5.8 %collective-permute-start.2 = (bf16[4,1,64,128]{3,2,1,0:T(8,128)(2,1)S(1)}, bf16[4,1,64,128]{3,2,1,0:T(8,128)(2,1)S(1)}, u32[]{:S(2)}, u32[]{:S(2)}) collective-permute-start(bf16[4,1,64,128]{3,2,1,0:T(8,128)(2,1)S(1)} %get-tuple-element.20), channel_id=1, source_target_pairs={{0,4},{4,8},{8,12},{1,5},{5,9},{9,13},{2,6},{6,10},{10,14},{3,7},{... | collective-permute-start | bytes 196616 | tf_op jit(solution)/shard_map/ppermute | solution.py:21
  16.1 6.2 %collective-permute-start.1 = (bf16[4,1,64,128]{3,2,1,0:T(8,128)(2,1)S(1)}, bf16[4,1,64,128]{3,2,1,0:T(8,128)(2,1)S(1)}, u32[]{:S(2)}, u32[]{:S(2)}) collective-permute-start(bf16[4,1,64,128]{3,2,1,0:T(8,128)(2,1)S(1)} %get-tuple-element.19), channel_id=1, source_target_pairs={{4,0},{8,4},{12,8},{5,1},{9,5},{13,9},{6,2},{10,6},{14,10},{7,3},{... | collective-permute-start | bytes 196616 | tf_op jit(solution)/shard_map/ppermute | solution.py:23
  28.5 1.4 copy-start.11
  29.8 14.5 %copy-start.12 = (u32[256]{0:T(256)S(1)}, u32[256]{0:T(256)}, u32[]{:S(2)}) copy-start(u32[256]{0:T(256)} %constant.34) | copy-start | bytes 3076
  29.9 86.3 %all-gather.2.cloned.1.call-start = ((), (), s32[]{:S(2)}) async-start(), calls=%async_computation.1 | async-start | bytes 1966080 | tf_op jit(solution)/shard_map/all_gather | solution.py:109
  29.9 4.0 collective-permute-start.3
  34.0 5.3 %collective-permute-start.4 = (bf16[4,1,64,128]{3,2,1,0:T(8,128)(2,1)S(1)}, bf16[4,1,64,128]{3,2,1,0:T(8,128)(2,1)S(1)}, u32[]{:S(2)}, u32[]{:S(2)}) collective-permute-start(bf16[4,1,64,128]{3,2,1,0:T(8,128)(2,1)S(1)} %get-tuple-element.17), channel_id=1, source_target_pairs={{0,4},{4,8},{8,12},{1,5},{5,9},{9,13},{2,6},{6,10},{10,14},{3,7},{... | collective-permute-start | bytes 196616 | tf_op jit(solution)/shard_map/ppermute | solution.py:21
  37.4 6.2 %collective-permute-start.5 = (bf16[4,1,64,128]{3,2,1,0:T(8,128)(2,1)S(1)}, bf16[4,1,64,128]{3,2,1,0:T(8,128)(2,1)S(1)}, u32[]{:S(2)}, u32[]{:S(2)}) collective-permute-start(bf16[4,1,64,128]{3,2,1,0:T(8,128)(2,1)S(1)} %get-tuple-element.18), channel_id=1, source_target_pairs={{4,0},{8,4},{12,8},{5,1},{9,5},{13,9},{6,2},{10,6},{14,10},{7,3},{... | collective-permute-start | bytes 196616 | tf_op jit(solution)/shard_map/ppermute | solution.py:23
  116.2 2.8 copy-start
  117.6 3.3 copy-start.4
  126.2 19.6 %collective-permute-start.6 = (bf16[2,4,64,128]{3,2,1,0:T(8,128)(2,1)S(1)}, bf16[2,4,64,128]{3,2,1,0:T(8,128)(2,1)S(1)}, u32[]{:S(2)}, u32[]{:S(2)}) collective-permute-start(bf16[2,4,64,128]{3,2,1,0:T(8,128)(2,1)S(1)} %get-tuple-element.14), channel_id=1, source_target_pairs={{16,0},{32,16},{48,32},{64,48},{80,64},{96,80},{112,96},{128,112},... | collective-permute-start | bytes 393224 | tf_op jit(solution)/shard_map/ppermute | solution.py:10
  132.3 32.5 %all-to-all-start = ((bf16[4,2,4,64,128]{4,3,2,1,0:T(8,128)(2,1)}), bf16[4,2,4,64,128]{4,3,2,1,0:T(8,128)(2,1)}, u32[]{:S(2)}, u32[]{:S(2)}) async-start(bf16[4,2,4,64,128]{4,3,2,1,0:T(8,128)(2,1)} %stack.203), calls=%async_computation | async-start | bytes 1048576 | tf_op jit(solution)/shard_map/all_to_all | solution.py:116
  138.0 75.4 %all-reduce.19.cloned.1.call-start = ((), (), s32[]{:S(2)}) async-start(), calls=%async_computation.3 | async-start | bytes 1048576
  144.6 6.1 %copy-start.5 = (bf16[64,3,3,3,256]{4,0,3,2,1:T(8,128)(2,1)S(1)}, bf16[64,3,3,3,256]{4,0,3,2,1:T(8,128)(2,1)}, u32[]{:S(2)}) copy-start(bf16[64,3,3,3,256]{4,0,3,2,1:T(8,128)(2,1)} %param.6) | copy-start | bytes 2654212
  145.8 6.0 %copy-start.9 = (f32[64,27,256]{2,0,1:T(8,128)}, f32[64,27,256]{2,0,1:T(8,128)S(1)}, u32[]{:S(2)}) copy-start(f32[64,27,256]{2,0,1:T(8,128)S(1)} %fusion.70) | copy-start | bytes 5308420
  145.8 6.9 %collective-permute-start.8 = (bf16[4,1,64,128]{3,2,1,0:T(8,128)(2,1)S(1)}, bf16[4,1,64,128]{3,2,1,0:T(8,128)(2,1)S(1)}, u32[]{:S(2)}, u32[]{:S(2)}) collective-permute-start(bf16[4,1,64,128]{3,2,1,0:T(8,128)(2,1)S(1)} %get-tuple-element.15), channel_id=1, source_target_pairs={{0,4},{4,8},{8,12},{1,5},{5,9},{9,13},{2,6},{6,10},{10,14},{3,7},{... | collective-permute-start | bytes 196616 | tf_op jit(solution)/shard_map/ppermute | solution.py:21
  149.2 6.5 %collective-permute-start.7 = (bf16[4,1,64,128]{3,2,1,0:T(8,128)(2,1)S(1)}, bf16[4,1,64,128]{3,2,1,0:T(8,128)(2,1)S(1)}, u32[]{:S(2)}, u32[]{:S(2)}) collective-permute-start(bf16[4,1,64,128]{3,2,1,0:T(8,128)(2,1)S(1)} %get-tuple-element.16), channel_id=1, source_target_pairs={{4,0},{8,4},{12,8},{5,1},{9,5},{13,9},{6,2},{10,6},{14,10},{7,3},{... | collective-permute-start | bytes 196616 | tf_op jit(solution)/shard_map/ppermute | solution.py:23
  158.0 1.2 copy-start.3
  159.8 1.2 copy-start.2
  161.0 1.2 copy-start.1
  164.8 247.5 %all-reduce.21.cloned.1.call-start = ((), (), s32[]{:S(2)}) async-start(), calls=%async_computation.4 | async-start | bytes 7077888 | tf_op jit(solution)/shard_map/psum | solution.py:134
  173.6 1.2 copy-start.7
  412.3 3.0 copy-start.8
Sparse Core Ops, SparseCore 0:
  30.0 53.8 all-reduce.16
  86.4 29.7 all-gather.1
  164.9 48.4 all-reduce.18
  217.8 194.5 all-reduce.20
